TPU v7x, 32 devices: a whole 2x2x4 slice. The times are simulated.
32 devices in a mesh: row: 4 (over z), col: 4 (over y, x), feat: 2 (over core).
Axes of the slice: x: 2, y: 2, z: 4, core: 2. Of those that a mesh axis runs over, the one named last changes fastest.
Arguments:
- tile_values: bfloat16 [4, 4, 80, 128, 128], P('row', 'col')
- tile_rows: int32 [4, 4, 80], P('row', 'col'), may hold values from 0 to 15, as said below
- tile_cols: int32 [4, 4, 80], P('row', 'col'), may hold values from 0 to 15
- tile_mask: int32 [4, 4, 80], P('row', 'col'), may hold values from 0 to 1, as said below
- degree_caps: int32 [8192], P(('row', 'col')), may hold values from 1 to 32, as said below
- clip_groups: int32 [8192], P(('row', 'col')), may hold values from 0 to 7
- clip_bounds: float32 [8], replicated, may hold values from 51.2 to 256
- features: bfloat16 [8192, 256], P('col', 'feat')
- weight: bfloat16 [256, 256], replicated, may hold values from -0.375 to 0.375
- out_grad: bfloat16 [8192, 256], P(('row', 'col'), 'feat')
- dp_noise: float32 [256, 256], P(None, 'feat'), may hold values from -6 to 6
Outputs:
- out_feat: bfloat16 [8192, 256], P(('row', 'col'), 'feat')
- grad_weight: float32 [256, 256], P(None, 'feat')
- grad_input: bfloat16 [8192, 256], P('col', 'feat')
Inputs may be any that keep to these rules, and one draw needn't show every extreme that they name: `tile_rows`: each tile slot of one pair of row and col indices names a distinct pair of block row and block column. `tile_mask`: at most all 80 slots of one pair of row and col indices are live; in every draw some pair has all of them live. degree_caps[i] is the number of nonzero entries in row i of A, raised to 1 where it is 0 and capped at 32.
All inputs are finite; a program needn't handle non-finite values.
Results may differ from a plain program's by a relative error of at most 0.006.
Values may be sent and summed in bfloat16 or wider, within the bound.
A program may use at most 128 MiB of HBM per device.

v0:
```python
import math

import jax
import jax.numpy as jnp
from jax import lax
from jax.sharding import PartitionSpec as P


def slot_products(tile_vals, take_ids, source, flipped):
    contraction = "kji,kjf->kif" if flipped else "kij,kjf->kif"
    slot_total = tile_vals.shape[0]
    picked = jnp.take(source, take_ids, axis=0)
    products = jnp.einsum(contraction, tile_vals, picked, preferred_element_type=jnp.float32)
    return (products, jnp.arange(slot_total, dtype=jnp.int32))


def block_sums(products, put_ids, live_slots, block_count):
    wanted = jnp.arange(block_count, dtype=jnp.int32)
    selector = ((put_ids[:, None] == wanted[None, :]) & live_slots[:, None]).astype(jnp.float32)
    return jnp.einsum("kb,kif->bif", selector, products, precision=lax.Precision.HIGHEST)


def per_device(
    tile_values,
    tile_rows,
    tile_cols,
    tile_mask,
    degree_caps,
    clip_groups,
    clip_bounds,
    features,
    weight,
    out_grad,
    dp_noise,
):
    tile_vals = tile_values[0, 0]
    row_ids = tile_rows[0, 0]
    col_ids = tile_cols[0, 0]
    tile_live = tile_mask[0, 0]
    block_size = tile_vals.shape[1]
    half_width = features.shape[1]
    node_count = out_grad.shape[0]
    col_devices = lax.axis_size("col")
    row_devices = lax.axis_size("row")
    row_blocks = node_count * col_devices // block_size
    col_blocks = features.shape[0] // block_size
    grad_scale = 1.0 / math.sqrt(node_count * col_devices * row_devices)
    source = features.reshape(col_blocks, block_size, half_width)
    products, order = slot_products(tile_vals, col_ids, source, False)
    put_rows = jnp.take(row_ids, order)
    live_rows = jnp.take(tile_live, order) == 1
    partial_value = block_sums(products, put_rows, live_rows, row_blocks)
    partial_value = partial_value.reshape(row_blocks * block_size, half_width)
    summed = lax.psum_scatter(partial_value, "col", scatter_dimension=0, tiled=True)
    node_scale = lax.rsqrt(degree_caps.astype(jnp.float32))[:, None]
    agg_half = (summed * node_scale).astype(jnp.bfloat16)
    aggregate = lax.all_gather(agg_half, "feat", axis=1, tiled=True)
    feat_idx = lax.axis_index("feat")
    weight_cols = lax.dynamic_slice_in_dim(weight, feat_idx * half_width, half_width, 1)
    weight_rows = lax.dynamic_slice_in_dim(weight, feat_idx * half_width, half_width, 0)
    pre_act = jnp.dot(aggregate, weight_cols, preferred_element_type=jnp.float32)
    out_feat = jax.nn.silu(pre_act).astype(jnp.bfloat16)
    gate_sig = jax.nn.sigmoid(pre_act)
    grad_pre = (
        out_grad.astype(jnp.float32) * gate_sig * (1.0 + pre_act * (1.0 - gate_sig))
    ).astype(jnp.bfloat16)
    grad_full = lax.all_gather(grad_pre, "feat", axis=1, tiled=True)
    agg_sq = jnp.sum(jnp.square(aggregate.astype(jnp.float32)), axis=1)
    grad_sq = jnp.sum(jnp.square(grad_full.astype(jnp.float32)), axis=1)
    group_hits = (
        clip_groups[:, None] == jnp.arange(clip_bounds.shape[0], dtype=jnp.int32)[None, :]
    ).astype(jnp.float32)
    bounds = jnp.sum(group_hits * clip_bounds[None, :], axis=1)
    factor = jnp.minimum(1.0, bounds / (jnp.sqrt(agg_sq + 1e-06) * jnp.sqrt(grad_sq + 1e-06)))
    clipped = (factor[:, None] * grad_pre.astype(jnp.float32)).astype(jnp.bfloat16)
    local_grad = lax.dot_general(
        aggregate, clipped, (((0,), (0,)), ((), ())), preferred_element_type=jnp.float32
    )
    grad_weight = lax.psum(local_grad, ("row", "col")) * grad_scale + dp_noise
    back_prod = lax.dot_general(
        grad_full, weight_rows, (((1,), (1,)), ((), ())), preferred_element_type=jnp.float32
    )
    grad_agg = (back_prod * node_scale).astype(jnp.bfloat16)
    range_grads = lax.all_gather(grad_agg, "col", axis=0, tiled=True)
    grad_source = range_grads.reshape(row_blocks, block_size, half_width)
    back_products, back_order = slot_products(tile_vals, row_ids, grad_source, True)
    put_cols = jnp.take(col_ids, back_order)
    live_cols = jnp.take(tile_live, back_order) == 1
    input_part = block_sums(back_products, put_cols, live_cols, col_blocks)
    input_part = input_part.reshape(col_blocks * block_size, half_width)
    grad_input = lax.psum(input_part, "row").astype(jnp.bfloat16)
    return (out_feat, grad_weight, grad_input)


def solution(mesh):
    placed = (
        P("row", "col", None, None, None),
        P("row", "col", None),
        P("row", "col", None),
        P("row", "col", None),
        P(("row", "col")),
        P(("row", "col")),
        P(),
        P("col", "feat"),
        P(),
        P(("row", "col"), "feat"),
        P(None, "feat"),
    )
    return jax.shard_map(
        per_device,
        mesh=mesh,
        in_specs=placed,
        out_specs=(P(("row", "col"), "feat"), P(None, "feat"), P("col", "feat")),
        check_vma=False,
    )
```

profile of v0, /device:TPU:0, one launch (start us, length us, event | category | flops | bytes accessed | tf_op | source)
XLA Modules:
  0.0 184.9 jit_solution(5821199909000592426)
XLA Ops:
  7.2 0.9 compare_and_fusion.1
  8.8 1.6 gather_fusion.1
  10.4 1.6 gather_fusion
  12.0 2.5 %gather_fusion.2 = bf16[80,128,128]{2,1,0:T(8,128)(2,1)} fusion(bf16[16,128,128]{2,1,0:T(8,128)(2,1)S(1)} %bitcast.41, s32[1024]{0:T(1024)S(1)} %pad_clamp_fusion.1), kind=kCustom, calls=%fused_computation.1.clone | custom fusion | bytes 5243200 | tf_op jit(solution)/shard_map/jit(_take)/gather | solution.py:12
  14.6 6.2 %fusion.8 = f32[80,128,128]{1,2,0:T(8,128)} fusion(bf16[1,1,80,128,128]{4,3,2,1,0:T(8,128)(2,1)S(1)} %copy-done, bf16[80,128,128]{2,1,0:T(8,128)(2,1)} %gather_fusion.2, pred[80]{0:T(512)(128)(4,1)S(1)} %compare_and_fusion.1), kind=kOutput, calls=%fused_computation.13 | convolution fusion | flops 336855040 | bytes 10485840 | tf_op jit(solution)/shard_map/kij,kjf->kif/dot_general | solution.py:13
  20.7 6.4 %copy.21 = f32[80,128,128]{2,0,1:T(8,128)} copy(f32[80,128,128]{1,2,0:T(8,128)} %fusion.8) | data formatting | bytes 10485760 | tf_op jit(solution)/shard_map/kij,kjf->kif/dot_general | solution.py:13
  27.1 4.3 %fusion.28 = f32[16,128,128]{2,0,1:T(8,128)S(1)} fusion(f32[80,128,128]{2,0,1:T(8,128)} %copy.21, s32[80]{0:T(128)S(1)} %broadcast_select_fusion.1, pred[80]{0:T(512)(128)(4,1)S(1)} %select_compare_fusion), kind=kOutput, calls=%fused_computation.38 | convolution fusion | flops 251660800 | bytes 6291856 | tf_op jit(solution)/shard_map/kb,kif->bif/dot_general | solution.py:20
  31.5 1.3 copy.22
  32.9 1.2 gather_fusion.3
  34.3 29.1 %reduce-scatter.2.cloned.1.call-done = f32[512,128]{1,0:T(8,128)} async-done(((f32[2048,128]{1,0:T(8,128)}), f32[512,128]{1,0:T(8,128)}) %reduce-scatter.2.cloned.1.call-update) | async-done | bytes 262160 | tf_op jit(solution)/shard_map/reduce_scatter | solution.py:54
  63.4 1.1 multiply_convert_fusion.3
  64.5 2.0 %all_gather.9 = bf16[512,256]{1,0:T(8,128)(2,1)S(1)} all-gather(bf16[512,128]{1,0:T(8,128)(2,1)S(1)} %multiply_convert_fusion.3), channel_id=1, replica_groups=mesh['row'=4,'col'=4,'feat'=2] {'feat'}, dimensions={1}, use_global_device_ids=true | all-gather | bytes 393216 | tf_op jit(solution)/shard_map/all_gather | solution.py:57
  66.7 1.0 multiply_convert_fusion.1
  67.7 2.0 %all_gather.10 = bf16[512,256]{1,0:T(8,128)(2,1)S(1)} all-gather(bf16[512,128]{1,0:T(8,128)(2,1)S(1)} %get-tuple-element.5), channel_id=1, replica_groups=mesh['row'=4,'col'=4,'feat'=2] {'feat'}, dimensions={1}, use_global_device_ids=true | all-gather | bytes 393216 | tf_op jit(solution)/shard_map/all_gather | solution.py:67
  70.0 1.0 fusion.21
  71.1 10.2 %all_gather.11 = bf16[2048,128]{1,0:T(8,128)(2,1)S(1)} all-gather(bf16[512,128]{1,0:T(8,128)(2,1)S(1)} %fusion.20), channel_id=1, replica_groups=mesh['row'=4,'col'=4,'feat'=2] {'col'}, dimensions={0}, use_global_device_ids=true | all-gather | bytes 655360 | tf_op jit(solution)/shard_map/all_gather | solution.py:84
  81.3 2.5 %gather_fusion.4 = bf16[80,128,128]{2,1,0:T(8,128)(2,1)} fusion(bf16[16,128,128]{2,1,0:T(8,128)(2,1)S(1)} %bitcast.40, s32[1024]{0:T(1024)S(1)} %pad_clamp_fusion), kind=kCustom, calls=%fused_computation.4.clone | custom fusion | bytes 5243200 | tf_op jit(solution)/shard_map/jit(_take)/gather | solution.py:12
  83.8 5.2 %fusion.13 = f32[80,128,128]{1,2,0:T(8,128)} fusion(bf16[1,1,80,128,128]{4,3,2,1,0:T(8,128)(2,1)S(1)} %copy-done, bf16[80,128,128]{2,1,0:T(8,128)(2,1)} %gather_fusion.4, pred[80]{0:T(512)(128)(4,1)S(1)} %compare_and_fusion), kind=kOutput, calls=%fused_computation.14 | convolution fusion | flops 336855040 | bytes 10485840 | tf_op jit(solution)/shard_map/kji,kjf->kif/dot_general | solution.py:13
  89.0 6.4 %copy.24 = f32[80,128,128]{2,0,1:T(8,128)} copy(f32[80,128,128]{1,2,0:T(8,128)} %fusion.13) | data formatting | bytes 10485760 | tf_op jit(solution)/shard_map/kji,kjf->kif/dot_general | solution.py:13
  95.4 4.3 %fusion.32 = f32[16,128,128]{2,0,1:T(8,128)S(1)} fusion(f32[80,128,128]{2,0,1:T(8,128)} %copy.24, s32[80]{0:T(128)S(1)} %broadcast_select_fusion, pred[80]{0:T(512)(128)(4,1)S(1)} %select_compare_fusion), kind=kOutput, calls=%fused_computation.41 | convolution fusion | flops 251660800 | bytes 6291856 | tf_op jit(solution)/shard_map/kb,kif->bif/dot_general | solution.py:20
  99.8 1.3 copy.25
  101.1 44.6 %all-reduce.4 = bf16[2048,128]{1,0:T(8,128)(2,1)} all-reduce(f32[2048,128]{1,0:T(8,128)} %bitcast.43), channel_id=1, replica_groups=mesh['row'=4,'col'=4,'feat'=2] {'row'}, use_global_device_ids=true, to_apply=%region_5.8 | all-reduce | flops 262144 | bytes 1572864 | tf_op jit(solution)/shard_map/psum | solution.py:91
  145.7 30.7 %all-reduce.3.cloned.1.call-done = f32[256,128]{1,0:T(8,128)} async-done(((f32[256,128]{1,0:T(8,128)}), f32[256,128]{1,0:T(8,128)}) %all-reduce.3.cloned.1.call-update) | async-done | bytes 131088 | tf_op jit(solution)/shard_map/psum | solution.py:79
  176.5 1.6 multiply_add_fusion
  (40 shorter events, 1.6 us)
Async XLA Ops:
  7.2 7.4 %copy-start = (bf16[1,1,80,128,128]{4,3,2,1,0:T(8,128)(2,1)S(1)}, bf16[1,1,80,128,128]{4,3,2,1,0:T(8,128)(2,1)}, u32[]{:S(2)}) copy-start(bf16[1,1,80,128,128]{4,3,2,1,0:T(8,128)(2,1)} %param.15) | copy-start | bytes 7864324
  7.2 4.8 %copy-start.3 = (bf16[2048,128]{1,0:T(8,128)(2,1)S(1)}, bf16[2048,128]{1,0:T(8,128)(2,1)}, u32[]{:S(2)}) copy-start(bf16[2048,128]{1,0:T(8,128)(2,1)} %param.22) | copy-start | bytes 1572868
  7.2 56.3 %reduce-scatter.2.cloned.1.call-start = ((), (), s32[]{:S(2)}) async-start(), calls=%async_computation.1 | async-start | bytes 1310720 | tf_op jit(solution)/shard_map/reduce_scatter | solution.py:54
  31.5 1.5 copy-start.1
  31.5 2.7 %copy-start.2 = (s32[1,1,80]{2,1,0:T(1,128)S(1)}, s32[1,1,80]{2,1,0:T(1,128)}, u32[]{:S(2)}) copy-start(s32[1,1,80]{2,1,0:T(1,128)} %param.16) | copy-start | bytes 964
  31.5 2.7 %copy-start.6 = (s32[512]{0:T(512)S(1)}, s32[512]{0:T(512)}, u32[]{:S(2)}) copy-start(s32[512]{0:T(512)} %param.20) | copy-start | bytes 6148
  31.5 2.7 %copy-start.8 = (f32[8]{0:T(128)S(1)}, f32[8]{0:T(128)}, u32[]{:S(2)}) copy-start(f32[8]{0:T(128)} %param.21) | copy-start | bytes 100
  31.5 2.8 %copy-start.7 = (s32[512]{0:T(512)S(1)}, s32[512]{0:T(512)}, u32[]{:S(2)}) copy-start(s32[512]{0:T(512)} %param.19) | copy-start | bytes 6148
  31.5 35.2 %copy-start.5 = (bf16[256,256]{1,0:T(8,128)(2,1)S(1)}, bf16[256,256]{1,0:T(8,128)(2,1)}, u32[]{:S(2)}) copy-start(bf16[256,256]{1,0:T(8,128)(2,1)} %param.23) | copy-start | bytes 393220
  31.5 35.2 %copy-start.9 = (bf16[512,128]{1,0:T(8,128)(2,1)S(1)}, bf16[512,128]{1,0:T(8,128)(2,1)}, u32[]{:S(2)}) copy-start(bf16[512,128]{1,0:T(8,128)(2,1)} %param.24) | copy-start | bytes 393220
  32.9 143.6 %all-reduce.3.cloned.1.call-start = ((), (), s32[]{:S(2)}) async-start(), calls=%async_computation.2 | async-start | bytes 262144 | tf_op jit(solution)/shard_map/psum | solution.py:79
  99.8 76.7 %copy-start.4 = (f32[256,128]{1,0:T(8,128)S(1)}, f32[256,128]{1,0:T(8,128)}, u32[]{:S(2)}) copy-start(f32[256,128]{1,0:T(8,128)} %param.25) | copy-start | bytes 393220
Sparse Core Ops, SparseCore 0:
  33.0 30.4 reduce-scatter.1
  71.2 105.2 all-reduce.2
where the time goes:
time: 185 us
  waiting for transfers between devices  59.9 us (32%)
  blocking collectives  58.8 us (32%)
  local copies, waits for them, and re-layouts  24.9 us (13%)
  matrix products  22.3 us (12%)
  between operations  14.3 us (8%)
  other arithmetic  4.65 us (3%)
    psum x1, blocking collectives, per_device(): grad_input = lax.psum(input_part, 'row').astype(jnp.bfloat16)  44.6 us
    psum x1, waiting for transfers between devices, per_device(): grad_weight = lax.psum(local_grad, ('row', 'col')) * grad_scale + dp_noise  30.7 us
    reduce_scatter x1, waiting for transfers between devices, per_device(): lax.psum_scatter(partial_value, 'col', scatter_dimension=0, tiled=True)  29.1 us
    dot_general x2, local copies, waits for them, and re-layouts, slot_products(): jnp.einsum(contraction, tile_vals, picked, preferred_element_type=jnp.flo...  12.8 us
    dot_general x2, matrix products, slot_products(): jnp.einsum(contraction, tile_vals, picked, preferred_element_type=jnp.flo...  11.4 us
    all_gather x1, blocking collectives, per_device(): range_grads = lax.all_gather(grad_agg, 'col', axis=0, tiled=True)  10.2 us
    dot_general x2, matrix products, block_sums(): jnp.einsum('kb,kif->bif', selector, products, precision=lax.Precision.HIG...  8.69 us
    gather x2, local copies, waits for them, and re-layouts, slot_products(): picked = jnp.take(source, take_ids, axis=0)  5.08 us
  transfers between devices with their start and end apart: 2, of which 2 were waited for; matrix products, arithmetic and copies ran while one was open for 11% of the time, Pallas kernels for 0%

commit v1 on v0

v1 whole, which is shorter than its diff:
```python
import functools
import math

import jax
import jax.numpy as jnp
from jax import lax
from jax.experimental import pallas as pl
from jax.experimental.pallas import tpu as pltpu
from jax.sharding import PartitionSpec as P

MESH = pl.DeviceIdType.MESH
PIECE = 256
LAG = 2


def layer(
    n_row, n_col, scale, cached,
    map_ref, bounds_ref, tiles_hbm, feats, weight, out_grad, noise, caps, groups,
    out_feat, grad_weight, grad_input,
    tiles, dense, rs_send, rs_recv, own, og_peer, agg, grads, acc,
    w_local, w_col, w_row, w_all, z_left, z_right, z_send, z_sum,
    tile_sem, og_sem, agg_sem, rs_ssem, rs_rsem, ag_ssem, ag_rsem,
    wc_ssem, wc_rsem, wr_ssem, wr_rsem, wa_ssem, wa_rsem,
    z_ssem, zl_rsem, zr_rsem, fin_ssem, fin_rsem,
):
    row, col, feat = lax.axis_index("row"), lax.axis_index("col"), lax.axis_index("feat")
    other = 1 - feat
    slots, blk = tiles_hbm.shape[0], tiles_hbm.shape[1]
    node, half = out_grad.shape
    col_blocks = feats.shape[0] // blk
    sub = node // blk
    w_rows = w_col.shape[1]
    pieces = z_send.shape[0]

    def remote(src, dst, ssem, rsem, where):
        return pltpu.make_async_remote_copy(
            src_ref=src, dst_ref=dst, send_sem=ssem, recv_sem=rsem,
            device_id=where, device_id_type=MESH,
        )

    load = pltpu.make_async_copy(tiles_hbm, tiles.at[pl.ds(0, slots)], tile_sem)
    load.start()

    barrier = pltpu.get_barrier_semaphore()
    pl.semaphore_signal(barrier, inc=1, device_id={"feat": other}, device_id_type=MESH)
    for step in range(1, n_col):
        pl.semaphore_signal(barrier, inc=1, device_id={"col": lax.rem(col + step, n_col)}, device_id_type=MESH)
    for step in range(1, n_row):
        pl.semaphore_signal(barrier, inc=1, device_id={"row": lax.rem(row + step, n_row)}, device_id_type=MESH)
    tiles[slots] = jnp.zeros((blk, blk), jnp.bfloat16)
    pl.semaphore_wait(barrier, n_col + n_row - 1)

    og_copy = remote(out_grad, og_peer, og_sem.at[0], og_sem.at[1], {"feat": other})
    og_copy.start()
    load.wait()

    def assemble(chunk, slot):
        for rb in range(sub):
            for cb in range(col_blocks):
                which = map_ref[(chunk * sub + rb) * col_blocks + cb]
                dense[slot, rb * blk:(rb + 1) * blk, cb * blk:(cb + 1) * blk] = tiles[which]

    def rs_copy(dest, sender):
        return remote(rs_send.at[dest], rs_recv.at[sender], rs_ssem.at[dest], rs_rsem.at[sender], {"col": dest})

    def forward(step, carry):
        chunk = lax.rem(col + 1 + step, n_col)
        slot = chunk if cached else 0
        assemble(chunk, slot)
        part = jnp.dot(dense[slot], feats[...], preferred_element_type=jnp.float32)

        @pl.when(step < n_col - 1)
        def _():
            rs_send[chunk] = part.astype(jnp.bfloat16)
            rs_copy(chunk, col).start()

        @pl.when(step == n_col - 1)
        def _():
            own[...] = part

        return carry

    lax.fori_loop(0, n_col, forward, 0)

    node_scale = jnp.transpose(jnp.broadcast_to(lax.rsqrt(caps[...].astype(jnp.float32)), (half, node)))
    bound = jnp.zeros((1, node), jnp.float32)
    for g in range(bounds_ref.shape[0]):
        bound = bound + jnp.where(groups[...] == g, bounds_ref[g], 0.0)
    bound = jnp.transpose(jnp.broadcast_to(bound, (half, node)))

    for step in range(1, n_col):
        peer = lax.rem(col - step + n_col, n_col)
        rs_copy(peer, peer).wait_recv()
        own[...] += rs_recv[peer].astype(jnp.float32)
    agg[feat] = (own[...] * node_scale).astype(jnp.bfloat16)
    agg_copy = remote(agg.at[feat], agg.at[feat], agg_sem.at[0], agg_sem.at[1], {"feat": other})
    agg_copy.start()
    og_copy.wait()
    agg_copy.wait()

    mine = pl.ds(pl.multiple_of(feat * half, half), half)
    theirs = pl.ds(pl.multiple_of(other * half, half), half)
    agg_0, agg_1 = agg[0], agg[1]

    def activation(columns):
        return jnp.dot(agg_0, weight[:half, columns], preferred_element_type=jnp.float32) + jnp.dot(
            agg_1, weight[half:, columns], preferred_element_type=jnp.float32
        )

    def gated(pre, cotangent):
        sig = 1.0 / (1.0 + jnp.exp(-pre))
        return sig, (cotangent.astype(jnp.float32) * sig * (1.0 + pre * (1.0 - sig))).astype(jnp.bfloat16)

    pre_mine = activation(mine)
    sig_mine, grad_mine = gated(pre_mine, out_grad[...])
    _, grad_theirs = gated(activation(theirs), og_peer[...])
    dims = (((1,), (1,)), ((), ()))
    back = lax.dot_general(grad_mine, weight[mine, mine], dims, preferred_element_type=jnp.float32)
    back += lax.dot_general(grad_theirs, weight[mine, theirs], dims, preferred_element_type=jnp.float32)
    grads[col] = jnp.transpose(back * node_scale).astype(jnp.bfloat16)

    def ag_copy(peer, sender):
        return remote(grads.at[sender], grads.at[sender], ag_ssem.at[peer], ag_rsem.at[sender], {"col": peer})

    for step in range(1, n_col):
        ag_copy(lax.rem(col + step, n_col), col).start()

    out_feat[...] = (pre_mine * sig_mine).astype(jnp.bfloat16)

    def squares(a, b):
        a, b = a.astype(jnp.float32), b.astype(jnp.float32)
        return jnp.sum(a * a + b * b, axis=1, keepdims=True)

    norm = jnp.sqrt(squares(agg_0, agg_1) + 1e-06) * jnp.sqrt(squares(grad_mine, grad_theirs) + 1e-06)
    factor = jnp.minimum(1.0, bound / norm)
    clipped = (factor * grad_mine.astype(jnp.float32)).astype(jnp.bfloat16)
    dims = (((0,), (0,)), ((), ()))
    w_local[:half] = lax.dot_general(agg_0, clipped, dims, preferred_element_type=jnp.float32)
    w_local[half:] = lax.dot_general(agg_1, clipped, dims, preferred_element_type=jnp.float32)

    def w_part(index):
        return w_local.at[pl.ds(pl.multiple_of(index * w_rows, w_rows), w_rows)]

    def wc_copy(dest, sender):
        return remote(w_part(dest), w_col.at[sender], wc_ssem.at[dest], wc_rsem.at[sender], {"col": dest})

    def wr_copy(dest, sender):
        return remote(w_row.at[sender], w_row.at[sender], wr_ssem.at[dest], wr_rsem.at[sender], {"row": dest})

    def wa_copy(dest, sender):
        return remote(w_all.at[sender], w_all.at[sender], wa_ssem.at[dest], wa_rsem.at[sender], {"col": dest})

    for step in range(1, n_col):
        wc_copy(lax.rem(col + step, n_col), col).start()

    def backward(peer):
        slot = peer if cached else 0
        if not cached:
            assemble(peer, slot)
        return jnp.dot(grads[peer], dense[slot], preferred_element_type=jnp.float32)

    acc[...] = backward(col)

    total = w_part(col)[...]
    for step in range(1, n_col):
        peer = lax.rem(col - step + n_col, n_col)
        wc_copy(peer, peer).wait_recv()
        total += w_col[peer]
    w_row[row] = total
    for step in range(1, n_row):
        wr_copy(lax.rem(row + step, n_row), row).start()

    def backward_step(step, carry):
        peer = lax.rem(col - step + n_col, n_col)
        ag_copy(peer, peer).wait_recv()
        acc[...] += backward(peer)
        return carry

    lax.fori_loop(1, n_col, backward_step, 0)

    def fold_rows():
        for step in range(1, n_row):
            peer = lax.rem(row - step + n_row, n_row)
            wr_copy(peer, peer).wait_recv()
        total = w_row[0]
        for index in range(1, n_row):
            total += w_row[index]
        w_all[col] = total
        for step in range(1, n_col):
            wa_copy(lax.rem(col + step, n_col), col).start()

    def middle(p):
        return n_row // 2 - 1 if p % 2 == 0 else n_row // 2

    def z_up(p):
        return remote(z_send.at[p], z_left.at[p], z_ssem.at[p], zl_rsem.at[p], {"row": row + 1})

    def z_down(p):
        return remote(z_send.at[p], z_right.at[p], z_ssem.at[p], zr_rsem.at[p], {"row": row - 1})

    def final(p, way):
        spot = grad_input.at[pl.ds(p * PIECE, PIECE)]
        return remote(spot, spot, fin_ssem.at[way, p], fin_rsem.at[p], {"row": row + 1 if way else row - 1})

    last = n_row - 1

    def reduce_piece(p):
        mid = middle(p)
        z_sum[...] = jnp.transpose(acc[:, p * PIECE:(p + 1) * PIECE])

        @pl.when((row <= mid) & (row > 0))
        def _():
            z_up(p).wait_recv()
            z_sum[...] += z_left[p].astype(jnp.float32)

        @pl.when((row >= mid) & (row < last))
        def _():
            z_down(p).wait_recv()
            z_sum[...] += z_right[p].astype(jnp.float32)

        @pl.when(row < mid)
        def _():
            z_send[p] = z_sum[...].astype(jnp.bfloat16)
            z_up(p).start()

        @pl.when(row > mid)
        def _():
            z_send[p] = z_sum[...].astype(jnp.bfloat16)
            z_down(p).start()

        @pl.when(row == mid)
        def _():
            grad_input[p * PIECE:(p + 1) * PIECE] = z_sum[...].astype(jnp.bfloat16)

        @pl.when((row == mid) & (row > 0))
        def _():
            final(p, 0).start()

        @pl.when((row == mid) & (row < last))
        def _():
            final(p, 1).start()

    def finish_piece(p):
        mid = middle(p)

        @pl.when(row != mid)
        def _():
            final(p, 0).wait_recv()

        @pl.when((row < mid) & (row > 0))
        def _():
            final(p, 0).start()

        @pl.when((row > mid) & (row < last))
        def _():
            final(p, 1).start()

    for p in range(pieces + LAG):
        if p < pieces:
            reduce_piece(p)
        if p == 1:
            fold_rows()
        if p >= LAG:
            finish_piece(p - LAG)

    for step in range(1, n_col):
        peer = lax.rem(col - step + n_col, n_col)
        wa_copy(peer, peer).wait_recv()
    for index in range(n_col):
        spot = pl.ds(index * w_rows, w_rows)
        grad_weight[spot] = w_all[index] * scale + noise[spot]

    for step in range(1, n_col):
        peer = lax.rem(col + step, n_col)
        rs_copy(peer, col).wait_send()
        ag_copy(peer, col).wait_send()
        wc_copy(peer, col).wait_send()
        wa_copy(peer, col).wait_send()
    for step in range(1, n_row):
        wr_copy(lax.rem(row + step, n_row), row).wait_send()
    for p in range(pieces):
        mid = middle(p)

        @pl.when(row < mid)
        def _():
            z_up(p).wait_send()

        @pl.when(row > mid)
        def _():
            z_down(p).wait_send()

        @pl.when((row <= mid) & (row > 0))
        def _():
            final(p, 0).wait_send()

        @pl.when((row >= mid) & (row < last))
        def _():
            final(p, 1).wait_send()


def per_device(
    tile_values, tile_rows, tile_cols, tile_mask, degree_caps, clip_groups,
    clip_bounds, features, weight, out_grad, dp_noise,
):
    tile_vals = tile_values[0, 0]
    slots, blk = tile_vals.shape[0], tile_vals.shape[1]
    node, half = out_grad.shape
    n_col, n_row = lax.axis_size("col"), lax.axis_size("row")
    col_range = features.shape[0]
    row_blocks, col_blocks = node * n_col // blk, col_range // blk
    hid = weight.shape[0]
    pair = jnp.where(tile_mask[0, 0] == 1, tile_rows[0, 0] * col_blocks + tile_cols[0, 0], -1)
    wanted = jnp.arange(row_blocks * col_blocks, dtype=jnp.int32)
    order = jnp.arange(slots, dtype=jnp.int32)
    slot_map = jnp.min(jnp.where(pair[:, None] == wanted[None, :], order[:, None], slots), axis=0)
    cached = row_blocks * col_blocks * blk * blk * 2 <= (20 << 20)
    pieces = col_range // PIECE
    bf16, f32 = jnp.bfloat16, jnp.float32
    vmem, smem = pl.BlockSpec(memory_space=pltpu.VMEM), pl.BlockSpec(memory_space=pltpu.SMEM)
    sem = pltpu.SemaphoreType.DMA
    call = pl.pallas_call(
        functools.partial(layer, n_row, n_col, 1.0 / math.sqrt(node * n_col * n_row), cached),
        out_shape=(
            jax.ShapeDtypeStruct((node, half), bf16),
            jax.ShapeDtypeStruct((hid, half), f32),
            jax.ShapeDtypeStruct((col_range, half), bf16),
        ),
        in_specs=[smem, smem, pl.BlockSpec(memory_space=pl.ANY)] + [vmem] * 6,
        out_specs=(vmem, vmem, vmem),
        scratch_shapes=[
            pltpu.VMEM((slots + 1, blk, blk), bf16),
            pltpu.VMEM((n_col if cached else 1, node, col_range), bf16),
            pltpu.VMEM((n_col, node, half), bf16),
            pltpu.VMEM((n_col, node, half), bf16),
            pltpu.VMEM((node, half), f32),
            pltpu.VMEM((node, half), bf16),
            pltpu.VMEM((2, node, half), bf16),
            pltpu.VMEM((n_col, half, node), bf16),
            pltpu.VMEM((half, col_range), f32),
            pltpu.VMEM((hid, half), f32),
            pltpu.VMEM((n_col, hid // n_col, half), f32),
            pltpu.VMEM((n_row, hid // n_col, half), f32),
            pltpu.VMEM((n_col, hid // n_col, half), f32),
            pltpu.VMEM((pieces, PIECE, half), bf16),
            pltpu.VMEM((pieces, PIECE, half), bf16),
            pltpu.VMEM((pieces, PIECE, half), bf16),
            pltpu.VMEM((PIECE, half), f32),
            sem, sem((2,)), sem((2,)),
            sem((n_col,)), sem((n_col,)), sem((n_col,)), sem((n_col,)),
            sem((n_col,)), sem((n_col,)), sem((n_row,)), sem((n_row,)),
            sem((n_col,)), sem((n_col,)),
            sem((pieces,)), sem((pieces,)), sem((pieces,)), sem((2, pieces)), sem((pieces,)),
        ],
        compiler_params=pltpu.CompilerParams(
            collective_id=0, has_side_effects=True, vmem_limit_bytes=56 << 20
        ),
        name="layer",
    )
    return call(
        slot_map, clip_bounds, tile_vals, features, weight, out_grad, dp_noise,
        degree_caps[None, :], clip_groups[None, :],
    )


def solution(mesh):
    placed = (
        P("row", "col", None, None, None),
        P("row", "col", None),
        P("row", "col", None),
        P("row", "col", None),
        P(("row", "col")),
        P(("row", "col")),
        P(),
        P("col", "feat"),
        P(),
        P(("row", "col"), "feat"),
        P(None, "feat"),
    )
    return jax.shard_map(
        per_device,
        mesh=mesh,
        in_specs=placed,
        out_specs=(P(("row", "col"), "feat"), P(None, "feat"), P("col", "feat")),
        check_vma=False,
    )
```

time: 185 us -> 81.3 us (0.44)
  Pallas kernels: 0 us -> 74.1 us
  waiting for transfers between devices: 59.9 us -> 0 us
  blocking collectives: 58.8 us -> 0 us
  matrix products: 22.3 us -> 0 us
  local copies, waits for them, and re-layouts: 24.9 us -> 5 us
  between operations: 14.3 us -> 0.64 us
  other arithmetic: 4.65 us -> 1.35 us
    pallas_call x0 -> x1, Pallas kernels: none -> 74.1 us  [per_device(): call(slot_map, clip_bounds, tile_vals, features, weight, out_grad, dp_noi...]
    psum x1 -> x0, blocking collectives: 44.6 us -> none  [per_device(): grad_input = lax.psum(input_part, 'row').astype(jnp.bfloat16)]
    psum x1 -> x0, waiting for transfers between devices: 30.7 us -> none  [per_device(): grad_weight = lax.psum(local_grad, ('row', 'col')) * grad_scale + dp_noise]
    reduce_scatter x1 -> x0, waiting for transfers between devices: 29.1 us -> none  [per_device(): lax.psum_scatter(partial_value, 'col', scatter_dimension=0, tiled=True)]
    dot_general x7 -> x0, matrix products: 22.3 us -> none  [the longest x2 11.4 us: slot_products(): jnp.einsum(contraction, tile_vals, picked, preferred_element_type=jnp.flo...]
    dot_general x4 -> x0, local copies, waits for them, and re-layouts: 15.4 us -> none  [the longest x2 12.8 us: slot_products(): jnp.einsum(contraction, tile_vals, picked, preferred_element_type=jnp.flo...]
    all_gather x3 -> x0, blocking collectives: 14.2 us -> none  [the longest x1 10.2 us: per_device(): range_grads = lax.all_gather(grad_agg, 'col', axis=0, tiled=True)]
    gather x5 -> x0, local copies, waits for them, and re-layouts: 9.48 us -> none  [the longest x2 5.08 us: slot_products(): picked = jnp.take(source, take_ids, axis=0)]
  transfers between devices with their start and end apart: 2 -> 0, of which waited for: 2 -> 0; matrix products, arithmetic and copies ran while one was open for 11% -> 0% of each run, Pallas kernels for 0% -> 0%
where the time goes in v1:
time: 81.3 us; the launch traced here: 81.1 us
  Pallas kernels  74.1 us (91%)
  local copies, waits for them, and re-layouts  5 us (6%)
  other arithmetic  1.35 us (2%)
    pallas_call x1, Pallas kernels, per_device(): call(slot_map, clip_bounds, tile_vals, features, weight, out_grad, dp_noi...  74.1 us
    unnamed x3, local copies, waits for them, and re-layouts  5 us

profile of v1, /device:TPU:0, one launch (start us, length us, event | category | flops | bytes accessed | tf_op | source)
XLA Modules:
  0.0 81.1 jit_solution(14667400917039555825)
XLA Ops:
  0.6 0.7 fusion
  1.3 0.7 select_reduce_fusion.map_ref
  2.0 74.1 %layer.1 = (bf16[512,128]{1,0:T(8,128)(2,1)}, f32[256,128]{1,0:T(8,128)}, bf16[2048,128]{1,0:T(8,128)(2,1)}) custom-call(s32[256]{0:T(256)} %select_reduce_fusion.map_ref, f32[8]{0:T(128)} %bounds_ref.1, bf16[80,128,128]{2,1,0:T(8,128)(2,1)} %bitcast.5, bf16[2048,128]{1,0:T(8,128)(2,1)} %feats.1, bf16[256,256]{1,0:T(8,128)(2,1)} %weight.1, ...), custom_call_target="tpu_custom_call" | custom-call | tf_op jit(solution)/shard_map/layer/pallas_call | solution.py:359
  76.1 1.6 %copy.17 = bf16[512,128]{1,0:T(8,128)(2,1)} copy(bf16[512,128]{1,0:T(8,128)(2,1)} %get-tuple-element.6) | data formatting | bytes 262144
  77.6 1.6 %copy.18 = f32[256,128]{1,0:T(8,128)} copy(f32[256,128]{1,0:T(8,128)} %get-tuple-element.7) | data formatting | bytes 262144
  79.2 1.9 %copy.19 = bf16[2048,128]{1,0:T(8,128)(2,1)} copy(bf16[2048,128]{1,0:T(8,128)(2,1)} %get-tuple-element.8) | data formatting | bytes 1048576

commit v2 on v1

--- a/solution.py
+++ b/solution.py
@@ -10,23 +10,26 @@
 
 MESH = pl.DeviceIdType.MESH
 PIECE = 256
-LAG = 2
+LEAD = 1
+LAG = 1
+LOADS = 4
 
 
 def layer(
     n_row, n_col, scale, cached,
-    map_ref, bounds_ref, tiles_hbm, feats, weight, out_grad, noise, caps, groups,
-    out_feat, grad_weight, grad_input,
+    map_ref, bounds_ref, tiles_hbm, feats_hbm, weight_hbm, og_hbm, noise_hbm, caps, groups,
+    out_feat_hbm, grad_weight_hbm, grad_input_hbm,
+    feats, weight, out_grad, noise, out_feat, grad_weight, grad_input,
     tiles, dense, rs_send, rs_recv, own, og_peer, agg, grads, acc,
     w_local, w_col, w_row, w_all, z_left, z_right, z_send, z_sum,
-    tile_sem, og_sem, agg_sem, rs_ssem, rs_rsem, ag_ssem, ag_rsem,
+    tile_sem, in_sem, out_sem, gin_sem, og_sem, agg_sem, rs_ssem, rs_rsem, ag_ssem, ag_rsem,
     wc_ssem, wc_rsem, wr_ssem, wr_rsem, wa_ssem, wa_rsem,
     z_ssem, zl_rsem, zr_rsem, fin_ssem, fin_rsem,
 ):
     row, col, feat = lax.axis_index("row"), lax.axis_index("col"), lax.axis_index("feat")
     other = 1 - feat
     slots, blk = tiles_hbm.shape[0], tiles_hbm.shape[1]
-    node, half = out_grad.shape
+    node, half = og_hbm.shape
     col_blocks = feats.shape[0] // blk
     sub = node // blk
     w_rows = w_col.shape[1]
@@ -38,8 +41,21 @@
             device_id=where, device_id_type=MESH,
         )
 
-    load = pltpu.make_async_copy(tiles_hbm, tiles.at[pl.ds(0, slots)], tile_sem)
-    load.start()
+    count = slots // LOADS
+    loads = [
+        pltpu.make_async_copy(
+            tiles_hbm.at[pl.ds(i * count, count)], tiles.at[pl.ds(i * count, count)], tile_sem.at[i]
+        )
+        for i in range(LOADS)
+    ]
+    inputs = [
+        pltpu.make_async_copy(src, dst, in_sem.at[i])
+        for i, (src, dst) in enumerate(
+            ((feats_hbm, feats), (og_hbm, out_grad), (weight_hbm, weight), (noise_hbm, noise))
+        )
+    ]
+    for copy in loads + inputs:
+        copy.start()
 
     barrier = pltpu.get_barrier_semaphore()
     pl.semaphore_signal(barrier, inc=1, device_id={"feat": other}, device_id_type=MESH)
@@ -50,9 +66,10 @@
     tiles[slots] = jnp.zeros((blk, blk), jnp.bfloat16)
     pl.semaphore_wait(barrier, n_col + n_row - 1)
 
-    og_copy = remote(out_grad, og_peer, og_sem.at[0], og_sem.at[1], {"feat": other})
+    og_copy = remote(og_hbm, og_peer, og_sem.at[0], og_sem.at[1], {"feat": other})
     og_copy.start()
-    load.wait()
+    for copy in loads + inputs:
+        copy.wait()
 
     def assemble(chunk, slot):
         for rb in range(sub):
@@ -126,6 +143,8 @@
         ag_copy(lax.rem(col + step, n_col), col).start()
 
     out_feat[...] = (pre_mine * sig_mine).astype(jnp.bfloat16)
+    feat_out = pltpu.make_async_copy(out_feat, out_feat_hbm, out_sem.at[0])
+    feat_out.start()
 
     def squares(a, b):
         a, b = a.astype(jnp.float32), b.astype(jnp.float32)
@@ -176,7 +195,13 @@
         acc[...] += backward(peer)
         return carry
 
-    lax.fori_loop(1, n_col, backward_step, 0)
+    lax.fori_loop(1, n_col - 1, backward_step, 0)
+
+    tail = lax.rem(col + 1, n_col)
+    tail_slot = tail if cached else 0
+    if not cached:
+        assemble(tail, tail_slot)
+    ag_copy(tail, tail).wait_recv()
 
     def fold_rows():
         for step in range(1, n_row):
@@ -189,79 +214,119 @@
         for step in range(1, n_col):
             wa_copy(lax.rem(col + step, n_col), col).start()
 
-    def middle(p):
-        return n_row // 2 - 1 if p % 2 == 0 else n_row // 2
-
-    def z_up(p):
+    last = n_row - 1
+    pairs = pieces // 2
+    lower = row < n_row // 2
+    odd = jnp.where(lower, 1, 0)
+    mid = jnp.where(lower, n_row // 2 - 1, n_row // 2)
+    is_mid = row == mid
+
+    def span(p):
+        return pl.ds(pl.multiple_of(p * PIECE, PIECE), PIECE)
+
+    def send_up(p):
         return remote(z_send.at[p], z_left.at[p], z_ssem.at[p], zl_rsem.at[p], {"row": row + 1})
 
-    def z_down(p):
+    def send_down(p):
         return remote(z_send.at[p], z_right.at[p], z_ssem.at[p], zr_rsem.at[p], {"row": row - 1})
 
     def final(p, way):
-        spot = grad_input.at[pl.ds(p * PIECE, PIECE)]
+        spot = grad_input.at[p]
         return remote(spot, spot, fin_ssem.at[way, p], fin_rsem.at[p], {"row": row + 1 if way else row - 1})
 
-    last = n_row - 1
-
-    def reduce_piece(p):
-        mid = middle(p)
-        z_sum[...] = jnp.transpose(acc[:, p * PIECE:(p + 1) * PIECE])
-
-        @pl.when((row <= mid) & (row > 0))
-        def _():
-            z_up(p).wait_recv()
+    def store(p):
+        return pltpu.make_async_copy(grad_input.at[p], grad_input_hbm.at[span(p)], gin_sem.at[p])
+
+    def own_part(p):
+        product = jnp.dot(grads[tail], dense[tail_slot, :, span(p)], preferred_element_type=jnp.float32)
+        z_sum[...] = jnp.transpose(acc[:, span(p)] + product)
+
+    def add_left(p, when):
+        @pl.when(when)
+        def _():
+            send_up(p).wait_recv()
             z_sum[...] += z_left[p].astype(jnp.float32)
 
-        @pl.when((row >= mid) & (row < last))
-        def _():
-            z_down(p).wait_recv()
+    def add_right(p, when):
+        @pl.when(when)
+        def _():
+            send_down(p).wait_recv()
             z_sum[...] += z_right[p].astype(jnp.float32)
 
-        @pl.when(row < mid)
+    def pass_on(p, up, down):
+        @pl.when(up | down)
         def _():
             z_send[p] = z_sum[...].astype(jnp.bfloat16)
-            z_up(p).start()
-
-        @pl.when(row > mid)
-        def _():
-            z_send[p] = z_sum[...].astype(jnp.bfloat16)
-            z_down(p).start()
-
-        @pl.when(row == mid)
-        def _():
-            grad_input[p * PIECE:(p + 1) * PIECE] = z_sum[...].astype(jnp.bfloat16)
-
-        @pl.when((row == mid) & (row > 0))
+
+        @pl.when(up)
+        def _():
+            send_up(p).start()
+
+        @pl.when(down)
+        def _():
+            send_down(p).start()
+
+    def first_piece(j):
+        p = 2 * j + odd
+        own_part(p)
+        add_left(p, lower & (row > 0))
+        add_right(p, (row >= n_row // 2) & (row < last))
+        pass_on(p, lower, row >= n_row // 2)
+
+    def second_piece(j):
+        p = 2 * j + 1 - odd
+        own_part(p)
+        add_left(p, (row > 0) & (row <= n_row // 2))
+        add_right(p, (row < last) & (row >= n_row // 2 - 1))
+        pass_on(p, row < n_row // 2 - 1, row > n_row // 2)
+
+        @pl.when(is_mid)
+        def _():
+            grad_input[p] = z_sum[...].astype(jnp.bfloat16)
+
+        @pl.when(is_mid & (row < last))
+        def _():
+            final(p, 1).start()
+
+        @pl.when(is_mid & (row > 0))
         def _():
             final(p, 0).start()
 
-        @pl.when((row == mid) & (row < last))
+    def finish(p, wait):
+        @pl.when(wait)
+        def _():
+            final(p, 0).wait_recv()
+
+        @pl.when(wait & lower & (row > 0))
+        def _():
+            final(p, 0).start()
+
+        @pl.when(wait & (row >= n_row // 2) & (row < last))
         def _():
             final(p, 1).start()
 
-    def finish_piece(p):
-        mid = middle(p)
-
-        @pl.when(row != mid)
-        def _():
-            final(p, 0).wait_recv()
-
-        @pl.when((row < mid) & (row > 0))
-        def _():
-            final(p, 0).start()
-
-        @pl.when((row > mid) & (row < last))
-        def _():
-            final(p, 1).start()
-
-    for p in range(pieces + LAG):
-        if p < pieces:
-            reduce_piece(p)
-        if p == 1:
-            fold_rows()
-        if p >= LAG:
-            finish_piece(p - LAG)
+        store(p).start()
+
+    def z_step(j, carry):
+        @pl.when(j < pairs)
+        def _():
+            first_piece(j)
+
+        @pl.when((j >= LEAD) & (j < pairs + LEAD))
+        def _():
+            second_piece(j - LEAD)
+
+        @pl.when(j >= LEAD + LAG)
+        def _():
+            done = j - LEAD - LAG
+            finish(2 * done + odd, row >= 0)
+            finish(2 * done + 1 - odd, row != mid)
+
+        return carry
+
+    lax.fori_loop(0, 1, z_step, 0)
+    fold_rows()
+    lax.fori_loop(1, pairs + LEAD + LAG, z_step, 0)
 
     for step in range(1, n_col):
         peer = lax.rem(col - step + n_col, n_col)
@@ -269,6 +334,8 @@
     for index in range(n_col):
         spot = pl.ds(index * w_rows, w_rows)
         grad_weight[spot] = w_all[index] * scale + noise[spot]
+    weight_out = pltpu.make_async_copy(grad_weight, grad_weight_hbm, out_sem.at[1])
+    weight_out.start()
 
     for step in range(1, n_col):
         peer = lax.rem(col + step, n_col)
@@ -278,24 +345,41 @@
         wa_copy(peer, col).wait_send()
     for step in range(1, n_row):
         wr_copy(lax.rem(row + step, n_row), row).wait_send()
-    for p in range(pieces):
-        mid = middle(p)
-
-        @pl.when(row < mid)
-        def _():
-            z_up(p).wait_send()
-
-        @pl.when(row > mid)
-        def _():
-            z_down(p).wait_send()
-
-        @pl.when((row <= mid) & (row > 0))
-        def _():
-            final(p, 0).wait_send()
-
-        @pl.when((row >= mid) & (row < last))
-        def _():
-            final(p, 1).wait_send()
+
+    def drain(j, carry):
+        for p, passed, done in (
+            (2 * j + odd, row >= 0, row < 0),
+            (2 * j + 1 - odd, row != mid, is_mid),
+        ):
+            @pl.when(passed)
+            def _():
+                send_up(p).wait_send()
+
+            @pl.when((lower | done) & (row > 0))
+            def _():
+                final(p, 0).wait_send()
+
+            @pl.when(((row >= n_row // 2) | done) & (row < last))
+            def _():
+                final(p, 1).wait_send()
+
+            store(p).wait()
+        return carry
+
+    lax.fori_loop(0, pairs, drain, 0)
+    feat_out.wait()
+    weight_out.wait()
+
+
+def deliver(a_in, b_in, c_in, a_out, b_out, c_out, sems):
+    copies = [
+        pltpu.make_async_copy(src, dst, sems.at[i])
+        for i, (src, dst) in enumerate(((a_in, a_out), (b_in, b_out), (c_in, c_out)))
+    ]
+    for copy in copies:
+        copy.start()
+    for copy in copies:
+        copy.wait()
 
 
 def per_device(
@@ -317,17 +401,26 @@
     pieces = col_range // PIECE
     bf16, f32 = jnp.bfloat16, jnp.float32
     vmem, smem = pl.BlockSpec(memory_space=pltpu.VMEM), pl.BlockSpec(memory_space=pltpu.SMEM)
+    anywhere = pl.BlockSpec(memory_space=pl.ANY)
     sem = pltpu.SemaphoreType.DMA
+    shapes = (
+        jax.ShapeDtypeStruct((node, half), bf16),
+        jax.ShapeDtypeStruct((hid, half), f32),
+        jax.ShapeDtypeStruct((col_range, half), bf16),
+    )
     call = pl.pallas_call(
         functools.partial(layer, n_row, n_col, 1.0 / math.sqrt(node * n_col * n_row), cached),
-        out_shape=(
-            jax.ShapeDtypeStruct((node, half), bf16),
-            jax.ShapeDtypeStruct((hid, half), f32),
-            jax.ShapeDtypeStruct((col_range, half), bf16),
-        ),
-        in_specs=[smem, smem, pl.BlockSpec(memory_space=pl.ANY)] + [vmem] * 6,
-        out_specs=(vmem, vmem, vmem),
+        out_shape=shapes,
+        in_specs=[smem, smem] + [anywhere] * 5 + [vmem] * 2,
+        out_specs=[anywhere] * 3,
         scratch_shapes=[
+            pltpu.VMEM((col_range, half), bf16),
+            pltpu.VMEM((hid, hid), bf16),
+            pltpu.VMEM((node, half), bf16),
+            pltpu.VMEM((hid, half), f32),
+            pltpu.VMEM((node, half), bf16),
+            pltpu.VMEM((hid, half), f32),
+            pltpu.VMEM((pieces, PIECE, half), bf16),
             pltpu.VMEM((slots + 1, blk, blk), bf16),
             pltpu.VMEM((n_col if cached else 1, node, col_range), bf16),
             pltpu.VMEM((n_col, node, half), bf16),
@@ -345,7 +438,7 @@
             pltpu.VMEM((pieces, PIECE, half), bf16),
             pltpu.VMEM((pieces, PIECE, half), bf16),
             pltpu.VMEM((PIECE, half), f32),
-            sem, sem((2,)), sem((2,)),
+            sem((LOADS,)), sem((4,)), sem((2,)), sem((pieces,)), sem((2,)), sem((2,)),
             sem((n_col,)), sem((n_col,)), sem((n_col,)), sem((n_col,)),
             sem((n_col,)), sem((n_col,)), sem((n_row,)), sem((n_row,)),
             sem((n_col,)), sem((n_col,)),
@@ -356,10 +449,18 @@
         ),
         name="layer",
     )
-    return call(
+    results = call(
         slot_map, clip_bounds, tile_vals, features, weight, out_grad, dp_noise,
         degree_caps[None, :], clip_groups[None, :],
     )
+    return pl.pallas_call(
+        deliver,
+        out_shape=shapes,
+        in_specs=[anywhere] * 3,
+        out_specs=[anywhere] * 3,
+        scratch_shapes=[sem((3,))],
+        name="deliver",
+    )(*results)
 
 
 def solution(mesh):

time: 81.3 us -> 91.5 us (1.13)
  Pallas kernels: 74.1 us -> 89.3 us
  local copies, waits for them, and re-layouts: 5 us -> 0 us
    pallas_call x0 -> x1, Pallas kernels: none -> 25 us  [per_device(): pl.pallas_call(deliver, out_shape=shapes, in_specs=[anywhere] * 3, out_sp...]
    pallas_call x1, Pallas kernels: 74.1 us -> 64.4 us  [per_device(): call(slot_map, clip_bounds, tile_vals, features, weight, out_grad, dp_noi...]
    unnamed x3 -> x0, local copies, waits for them, and re-layouts: 5 us -> none
where the time goes in v2:
time: 91.5 us; the launch traced here: 91.3 us
  Pallas kernels  89.3 us (98%)
  other arithmetic  1.35 us (1%)
    pallas_call x1, Pallas kernels, per_device(): call(slot_map, clip_bounds, tile_vals, features, weight, out_grad, dp_noi...  64.4 us
    pallas_call x1, Pallas kernels, per_device(): pl.pallas_call(deliver, out_shape=shapes, in_specs=[anywhere] * 3, out_sp...  25 us

profile of v2, /device:TPU:0, one launch (start us, length us, event | category | flops | bytes accessed | tf_op | source)
XLA Modules:
  0.0 91.3 jit_solution(10475526047139432553)
XLA Ops:
  0.6 0.7 fusion
  1.3 0.7 select_reduce_fusion.map_ref
  2.0 64.4 %layer.1 = (bf16[512,128]{1,0:T(8,128)(2,1)}, f32[256,128]{1,0:T(8,128)}, bf16[2048,128]{1,0:T(8,128)(2,1)}) custom-call(s32[256]{0:T(256)} %select_reduce_fusion.map_ref, f32[8]{0:T(128)} %bounds_ref.1, bf16[80,128,128]{2,1,0:T(8,128)(2,1)} %bitcast.5, bf16[2048,128]{1,0:T(8,128)(2,1)} %feats_hbm.1, bf16[256,256]{1,0:T(8,128)(2,1)} %weight_hbm.1, ...), custom_call_target="tpu_custom_call" | custom-call | tf_op jit(solution)/shard_map/layer/pallas_call | solution.py:452
  66.4 25.0 %deliver.1 = (bf16[512,128]{1,0:T(8,128)(2,1)}, f32[256,128]{1,0:T(8,128)}, bf16[2048,128]{1,0:T(8,128)(2,1)}) custom-call(bf16[512,128]{1,0:T(8,128)(2,1)} %get-tuple-element.6.a_in, f32[256,128]{1,0:T(8,128)} %get-tuple-element.7.b_in, bf16[2048,128]{1,0:T(8,128)(2,1)} %get-tuple-element.8.c_in), custom_call_target="tpu_custom_call" | custom-call | tf_op jit(solution)/shard_map/deliver/pallas_call | solution.py:456

commit v3 on v2

--- a/solution.py
+++ b/solution.py
@@ -10,8 +10,8 @@
 
 MESH = pl.DeviceIdType.MESH
 PIECE = 256
-LEAD = 1
-LAG = 1
+LEAD = 2
+LAG = 3
 LOADS = 4
 
 
@@ -371,14 +371,16 @@
     weight_out.wait()
 
 
-def deliver(a_in, b_in, c_in, a_out, b_out, c_out, sems):
-    copies = [
-        pltpu.make_async_copy(src, dst, sems.at[i])
-        for i, (src, dst) in enumerate(((a_in, a_out), (b_in, b_out), (c_in, c_out)))
-    ]
-    for copy in copies:
+def deliver(a_in, b_in, c_in, a_out, b_out, c_out, a_buf, b_buf, c_buf, sems):
+    rows = ((a_in, a_buf, a_out), (b_in, b_buf, b_out), (c_in, c_buf, c_out))
+    loads = [pltpu.make_async_copy(src, buf, sems.at[0, i]) for i, (src, buf, _) in enumerate(rows)]
+    stores = [pltpu.make_async_copy(buf, dst, sems.at[1, i]) for i, (_, buf, dst) in enumerate(rows)]
+    for copy in loads:
         copy.start()
-    for copy in copies:
+    for load, store in zip(loads, stores):
+        load.wait()
+        store.start()
+    for copy in stores:
         copy.wait()
 
 
@@ -458,7 +460,7 @@
         out_shape=shapes,
         in_specs=[anywhere] * 3,
         out_specs=[anywhere] * 3,
-        scratch_shapes=[sem((3,))],
+        scratch_shapes=[pltpu.VMEM(x.shape, x.dtype) for x in shapes] + [sem((2, 3))],
         name="deliver",
     )(*results)
 

time: 91.5 us -> 55.8 us (0.61)
  Pallas kernels: 89.3 us -> 53.6 us
    pallas_call x1, Pallas kernels: 25 us -> 2.02 us  [per_device(): pl.pallas_call(deliver, out_shape=shapes, in_specs=[anywhere] * 3, out_sp...]
    pallas_call x1, Pallas kernels: 64.4 us -> 51.6 us  [per_device(): call(slot_map, clip_bounds, tile_vals, features, weight, out_grad, dp_noi...]
where the time goes in v3:
time: 55.8 us; the launch traced here: 55.6 us
  Pallas kernels  53.6 us (96%)
  other arithmetic  1.35 us (2%)
  between operations  0.64 us (1%)
    pallas_call x1, Pallas kernels, per_device(): call(slot_map, clip_bounds, tile_vals, features, weight, out_grad, dp_noi...  51.6 us
    pallas_call x1, Pallas kernels, per_device(): pl.pallas_call(deliver, out_shape=shapes, in_specs=[anywhere] * 3, out_sp...  2.02 us

profile of v3, /device:TPU:0, one launch (start us, length us, event | category | flops | bytes accessed | tf_op | source)
XLA Modules:
  0.0 55.6 jit_solution(7065249250433795713)
XLA Ops:
  0.6 0.7 %fusion = s32[80]{0:T(128)S(1)} fusion(s32[1,1,80]{2,1,0:T(1,128)} %param.14, s32[1,1,80]{2,1,0:T(1,128)} %param.13, s32[1,1,80]{2,1,0:T(1,128)} %param.12), kind=kLoop, calls=%fused_computation.3 | loop fusion | flops 320 | bytes 1280 | tf_op jit(solution)/shard_map/jit(_where)/select_n | solution.py:398
  1.3 0.7 %select_reduce_fusion.map_ref = s32[256]{0:T(256)} fusion(s32[80]{0:T(128)S(1)} %fusion), kind=kLoop, calls=%fused_computation | loop fusion | flops 61184 | bytes 1344 | tf_op jit(solution)/shard_map/reduce_min | solution.py:401
  2.0 51.6 %layer.1 = (bf16[512,128]{1,0:T(8,128)(2,1)}, f32[256,128]{1,0:T(8,128)}, bf16[2048,128]{1,0:T(8,128)(2,1)}) custom-call(s32[256]{0:T(256)} %select_reduce_fusion.map_ref, f32[8]{0:T(128)} %bounds_ref.1, bf16[80,128,128]{2,1,0:T(8,128)(2,1)} %bitcast.5, bf16[2048,128]{1,0:T(8,128)(2,1)} %feats_hbm.1, bf16[256,256]{1,0:T(8,128)(2,1)} %weight_hbm.1, ...), custom_call_target="tpu_custom_call" | custom-call | tf_op jit(solution)/shard_map/layer/pallas_call | solution.py:454
  53.6 2.0 %deliver.1 = (bf16[512,128]{1,0:T(8,128)(2,1)}, f32[256,128]{1,0:T(8,128)}, bf16[2048,128]{1,0:T(8,128)(2,1)}) custom-call(bf16[512,128]{1,0:T(8,128)(2,1)} %get-tuple-element.6.a_in, f32[256,128]{1,0:T(8,128)} %get-tuple-element.7.b_in, bf16[2048,128]{1,0:T(8,128)(2,1)} %get-tuple-element.8.c_in), custom_call_target="tpu_custom_call" | custom-call | tf_op jit(solution)/shard_map/deliver/pallas_call | solution.py:458

commit v4 on v3

--- a/solution.py
+++ b/solution.py
@@ -67,8 +67,7 @@
     pl.semaphore_wait(barrier, n_col + n_row - 1)
 
     og_copy = remote(og_hbm, og_peer, og_sem.at[0], og_sem.at[1], {"feat": other})
-    og_copy.start()
-    for copy in loads + inputs:
+    for copy in loads + inputs[:1]:
         copy.wait()
 
     def assemble(chunk, slot):
@@ -98,6 +97,7 @@
         return carry
 
     lax.fori_loop(0, n_col, forward, 0)
+    og_copy.start()
 
     node_scale = jnp.transpose(jnp.broadcast_to(lax.rsqrt(caps[...].astype(jnp.float32)), (half, node)))
     bound = jnp.zeros((1, node), jnp.float32)
@@ -112,6 +112,8 @@
     agg[feat] = (own[...] * node_scale).astype(jnp.bfloat16)
     agg_copy = remote(agg.at[feat], agg.at[feat], agg_sem.at[0], agg_sem.at[1], {"feat": other})
     agg_copy.start()
+    for copy in inputs[1:]:
+        copy.wait()
     og_copy.wait()
     agg_copy.wait()
 

time: 55.8 us -> 55.8 us (level)
  no operation moved by 1% of the time
where the time goes in v4:
time: 55.8 us; the launch traced here: 55.6 us
  Pallas kernels  53.6 us (96%)
  other arithmetic  1.35 us (2%)
  between operations  0.64 us (1%)
    pallas_call x1, Pallas kernels, per_device(): call(slot_map, clip_bounds, tile_vals, features, weight, out_grad, dp_noi...  51.6 us
    pallas_call x1, Pallas kernels, per_device(): pl.pallas_call(deliver, out_shape=shapes, in_specs=[anywhere] * 3, out_sp...  2.02 us

profile of v4, /device:TPU:0, one launch (start us, length us, event | category | flops | bytes accessed | tf_op | source)
XLA Modules:
  0.0 55.6 jit_solution(17340145936134257880)
XLA Ops:
  0.6 0.7 %fusion = s32[80]{0:T(128)S(1)} fusion(s32[1,1,80]{2,1,0:T(1,128)} %param.14, s32[1,1,80]{2,1,0:T(1,128)} %param.13, s32[1,1,80]{2,1,0:T(1,128)} %param.12), kind=kLoop, calls=%fused_computation.3 | loop fusion | flops 320 | bytes 1280 | tf_op jit(solution)/shard_map/jit(_where)/select_n | solution.py:400
  1.3 0.7 %select_reduce_fusion.map_ref = s32[256]{0:T(256)} fusion(s32[80]{0:T(128)S(1)} %fusion), kind=kLoop, calls=%fused_computation | loop fusion | flops 61184 | bytes 1344 | tf_op jit(solution)/shard_map/reduce_min | solution.py:403
  2.0 51.6 %layer.1 = (bf16[512,128]{1,0:T(8,128)(2,1)}, f32[256,128]{1,0:T(8,128)}, bf16[2048,128]{1,0:T(8,128)(2,1)}) custom-call(s32[256]{0:T(256)} %select_reduce_fusion.map_ref, f32[8]{0:T(128)} %bounds_ref.1, bf16[80,128,128]{2,1,0:T(8,128)(2,1)} %bitcast.5, bf16[2048,128]{1,0:T(8,128)(2,1)} %feats_hbm.1, bf16[256,256]{1,0:T(8,128)(2,1)} %weight_hbm.1, ...), custom_call_target="tpu_custom_call" | custom-call | tf_op jit(solution)/shard_map/layer/pallas_call | solution.py:456
  53.6 2.0 %deliver.1 = (bf16[512,128]{1,0:T(8,128)(2,1)}, f32[256,128]{1,0:T(8,128)}, bf16[2048,128]{1,0:T(8,128)(2,1)}) custom-call(bf16[512,128]{1,0:T(8,128)(2,1)} %get-tuple-element.6.a_in, f32[256,128]{1,0:T(8,128)} %get-tuple-element.7.b_in, bf16[2048,128]{1,0:T(8,128)(2,1)} %get-tuple-element.8.c_in), custom_call_target="tpu_custom_call" | custom-call | tf_op jit(solution)/shard_map/deliver/pallas_call | solution.py:460
